TPU v7x, 32 devices: a whole 2x2x4 slice. The times are simulated.
32 devices in a mesh: fsdp: 8 (over y, x, core), mode: 4 (over z).
Axes of the slice: x: 2, y: 2, z: 4, core: 2. Of those that a mesh axis runs over, the one named last changes fastest.
Arguments:
- gradient: float32 [32, 16, 2, 256, 512], P('mode', None, None, 'fsdp'), may hold values from -1000 to 1000, as said below
- start_in: float32 [512, 128], replicated, may hold values from -6 to 6
- start_out: float32 [256, 128], replicated, may hold values from -6 to 6
- start_x: float32 [32, 16], replicated, may hold values from -6 to 6
- start_y: float32 [16, 8], replicated, may hold values from -6 to 6
Outputs:
- factor_in: float32 [512, 128], P(('fsdp', 'mode'))
- factor_out: float32 [256, 128], P('fsdp')
- factor_x: float32 [32, 16], replicated
- factor_y: float32 [16, 8], replicated
- core: float32 [16, 128, 8, 2, 128], P('mode', 'fsdp')
Inputs may be any that keep to these rules, and one draw needn't show every extreme that they name: A weight gradient of one spectral layer, finite and bounded in magnitude.
All inputs are finite; a program needn't handle non-finite values.
Results may differ from a plain program's by a relative error of at most 0.0003.
Values sent between devices are 32-bit elements; how exact they have to be, the bound alone decides.
No kernel may reach another device: no remote copies, remote signals or barrier semaphores. Data moves between devices by JAX's collectives and lax.ppermute only.
A program may use at most 320 MiB of HBM per device.

v0:
```python
import jax
import jax.numpy as jnp
from jax import lax
from jax.sharding import PartitionSpec as P

I = 512
SWEEPS = 2
precise = lax.Precision.HIGHEST


def sweeps(gram, subspace):
    for sweep_index in range(SWEEPS):
        product = jnp.dot(gram, subspace, precision=precise)
        inner = jnp.dot(product.T, product, precision=precise)
        lower_factor = jnp.linalg.cholesky(inner)
        subspace = jax.scipy.linalg.solve_triangular(lower_factor, product.T, lower=True).T
    return subspace


def shards(gradient, start_in, start_out, start_x, start_y):
    fsdp_index = lax.axis_index("fsdp")
    mode_index = lax.axis_index("mode")
    joint_index = lax.axis_index(("fsdp", "mode"))
    fsdp_count = lax.axis_size("fsdp")
    mode_count = lax.axis_size("mode")
    rows_in = I // (fsdp_count * mode_count)
    local_first = gradient.shape[0]
    local_out = gradient.shape[3]
    gram_y_part = jnp.einsum("xycoi,xzcoi->yz", gradient, gradient, precision=precise)
    gram_in_part = jnp.einsum("xycoi,xycoj->ij", gradient, gradient, precision=precise)
    gram_in, gram_y = lax.psum((gram_in_part, gram_y_part), ("fsdp", "mode"))
    full_in = sweeps(gram_in, start_in)
    factor_y = sweeps(gram_y, start_y)
    by_out = lax.all_to_all(gradient, "fsdp", split_axis=4, concat_axis=3, tiled=True)
    gram_out = lax.psum(
        jnp.einsum("xycoi,xycpi->op", by_out, by_out, precision=precise), ("fsdp", "mode")
    )
    by_first = lax.all_to_all(gradient, "mode", split_axis=4, concat_axis=0, tiled=True)
    gram_x = lax.psum(
        jnp.einsum("xycoi,zycoi->xz", by_first, by_first, precision=precise), ("fsdp", "mode")
    )
    full_out = sweeps(gram_out, start_out)
    factor_x = sweeps(gram_x, start_x)
    partial_in = jnp.einsum("xycoi,ia->xycoa", gradient, full_in, precision=precise)
    out_rows = lax.dynamic_slice_in_dim(full_out, fsdp_index * local_out, local_out, 0)
    first_rows = lax.dynamic_slice_in_dim(factor_x, mode_index * local_first, local_first, 0)
    reduced = jnp.einsum("xycoa,yq->xqcoa", partial_in, factor_y, precision=precise)
    columns = first_rows
    partial_core = lax.psum_scatter(
        jnp.einsum("xqcoa,xp->pqcoa", reduced, columns, precision=precise),
        "mode",
        scatter_dimension=0,
        tiled=True,
    )
    columns = out_rows
    swapped = lax.psum_scatter(
        jnp.einsum("pqcoa,ob->bpqca", partial_core, columns, precision=precise),
        "fsdp",
        scatter_dimension=0,
        tiled=True,
    )
    core = jnp.transpose(swapped, (1, 0, 2, 3, 4))
    factor_in = lax.dynamic_slice_in_dim(full_in, joint_index * rows_in, rows_in, 0)
    return (factor_in, out_rows, factor_x, factor_y, core)


def solution(mesh):
    in_specs = (P("mode", None, None, "fsdp", None), P(), P(), P(), P())
    out_specs = (
        P(("fsdp", "mode"), None),
        P("fsdp", None),
        P(),
        P(),
        P("mode", "fsdp", None, None, None),
    )
    return jax.shard_map(shards, mesh=mesh, in_specs=in_specs, out_specs=out_specs, check_vma=False)
```

profile of v0, /device:TPU:0, one launch (start us, length us, event | category | flops | bytes accessed | tf_op | source)
XLA Modules:
  0.0 1270.9 jit_solution(15433066055648959006)
XLA Ops:
  7.2 50.4 %copy.78 = f32[8,16,2,32,512]{3,1,2,0,4:T(8,128)} copy(f32[8,16,2,32,512]{4,3,2,1,0:T(8,128)} %param.16) | data formatting | bytes 33554432 | tf_op args[0]
  57.6 67.0 %reshape.45 = f32[8,1,524288]{2,1,0:T(1,128)} reshape(f32[512,8,2,16,32]{4,3,2,1,0:T(8,128)} %bitcast.156) | data formatting | bytes 33554432
  124.6 5.7 all-to-all-start
  130.3 60.2 %reshape.47 = f32[4,1,1048576]{2,1,0:T(1,128)} reshape(f32[512,8,2,16,32]{4,3,2,1,0:T(8,128)} %bitcast.158) | data formatting | bytes 33554432
  190.5 124.4 %all-to-all-done = f32[8,1,524288]{2,1,0:T(1,128)} async-done(((f32[8,1,524288]{2,1,0:T(1,128)}), f32[8,1,524288]{2,1,0:T(1,128)}, u32[]{:S(2)}, u32[]{:S(2)}) %all-to-all-start) | async-done | bytes 16777248 | tf_op jit(solution)/shard_map/all_to_all | solution.py:34
  314.9 7.2 all-to-all-start.1
  322.2 31.6 %fusion.13 = f32[512,512]{1,0:T(8,128)} fusion(f32[8,16,2,32,512]{4,3,2,1,0:T(8,128)} %param.16), kind=kOutput, calls=%fused_computation.12 | convolution fusion | flops 25769803776 | bytes 17825792 | tf_op jit(solution)/shard_map/xycoi,xycoj->ij/dot_general | solution.py:30
  354.3 50.6 %reduce.12 = f32[8,524288]{1,0:T(8,128)} reduce(f32[8,1,524288]{2,1,0:T(1,128)} %all-to-all-done, f32[]{:T(128)} %broadcast.120), dimensions={1}, to_apply=%all_to_all.26.reduce_sub_computation | reduce | bytes 33554436 | tf_op jit(solution)/shard_map/all_to_all | solution.py:34
  404.9 55.4 %reshape.46 = f32[512,8,2,16,32]{4,3,2,1,0:T(8,128)} reshape(f32[8,524288]{1,0:T(8,128)} %reduce.12) | data formatting | bytes 33554432
  460.3 48.4 %copy.113 = f32[8,16,2,32,8,64]{5,3,4,1,0,2:T(8,128)} copy(f32[8,16,2,32,8,64]{3,1,2,0,5,4:T(8,128)} %bitcast.11) | data formatting | bytes 33554432 | tf_op jit(solution)/shard_map/all_to_all | solution.py:34
  508.7 36.8 %convolution_bitcast_fusion.1 = f32[256,256]{1,0:T(8,128)} fusion(f32[8,16,2,256,64]{4,3,1,0,2:T(8,128)} %bitcast.196), kind=kOutput, calls=%fused_computation.13 | convolution fusion | flops 12884901888 | bytes 17039360 | tf_op jit(solution)/shard_map/xycoi,xycpi->op/dot_general | solution.py:36
  545.6 51.9 %fusion.19 = f32[16,16]{1,0:T(8,128)S(1)} fusion(f32[8,16,2,32,512]{4,3,2,1,0:T(8,128)} %param.16), kind=kOutput, calls=%fused_computation.15 | convolution fusion | flops 805306368 | bytes 16778240 | tf_op jit(solution)/shard_map/xycoi,xzcoi->yz/dot_general | solution.py:29
  597.5 196.5 %all-reduce.4.cloned.1.call-done = (f32[512,512]{1,0:T(8,128)}, f32[256,256]{1,0:T(8,128)}) async-done(((f32[512,512]{1,0:T(8,128)}, f32[256,256]{1,0:T(8,128)}), (f32[512,512]{1,0:T(8,128)}, f32[256,256]{1,0:T(8,128)})) %all-reduce.4.cloned.1.call-update) | async-done | bytes 1310736 | tf_op jit(solution)/shard_map/psum | solution.py:31
  794.0 2.2 fusion.77
  796.2 0.6 fusion.78
  796.9 11.7 cholesky.158
  808.7 0.6 compare_reduce_fusion.7
  809.3 0.7 fusion.31
  810.0 9.8 custom-call.22
  820.2 2.2 fusion.79
  822.5 0.6 fusion.80
  823.2 11.9 cholesky.169
  835.1 0.6 compare_reduce_fusion.6
  835.7 0.7 fusion.32
  836.4 9.8 custom-call.23
  846.6 17.3 %convolution_bitcast_fusion = f32[8,16,2,32,128]{4,3,2,1,0:T(8,128)} fusion(f32[8,16,2,32,512]{4,3,2,1,0:T(8,128)} %param.16, f32[128,512]{1,0:T(8,128)S(1)} %fusion.23), kind=kOutput, calls=%fused_computation.8 | convolution fusion | flops 6442450944 | bytes 21233664 | tf_op jit(solution)/shard_map/xycoi,ia->xycoa/dot_general | solution.py:44
  864.0 54.5 %reduce.13 = f32[4,1048576]{1,0:T(4,128)} reduce(f32[4,1,1048576]{2,1,0:T(1,128)} %all-to-all-done.1, f32[]{:T(128)} %broadcast.120), dimensions={1}, to_apply=%all_to_all.30.reduce_sub_computation | reduce | bytes 33554436 | tf_op jit(solution)/shard_map/all_to_all | solution.py:38
  918.5 76.0 %reshape.48 = f32[512,8,2,16,32]{4,3,2,1,0:T(8,128)} reshape(f32[4,1048576]{1,0:T(4,128)} %reduce.13) | data formatting | bytes 33554432
  994.5 42.8 %copy.85 = f32[8,16,2,32,4,128]{5,0,4,1,3,2:T(8,128)} copy(f32[8,16,2,32,4,128]{3,1,2,0,5,4:T(8,128)} %bitcast.26) | data formatting | bytes 33554432 | tf_op jit(solution)/shard_map/all_to_all | solution.py:38
  1037.3 19.6 %fusion.16 = f32[32,32]{1,0:T(8,128)S(1)} fusion(f32[8,16,2,32,4,128]{5,0,4,1,3,2:T(8,128)} %copy.85), kind=kOutput, calls=%fused_computation.14 | convolution fusion | flops 1610612736 | bytes 16781312 | tf_op jit(solution)/shard_map/xycoi,zycoi->xz/dot_general | solution.py:40
  1057.0 39.5 %all-reduce = (f32[32,32]{1,0:T(8,128)S(1)}, f32[16,16]{1,0:T(8,128)S(1)}) all-reduce(f32[32,32]{1,0:T(8,128)S(1)} %fusion.16, f32[16,16]{1,0:T(8,128)S(1)} %fusion.19), channel_id=1, replica_groups=mesh['fsdp'=8,'mode'=4] {'fsdp','mode'}, use_global_device_ids=true, to_apply=%region_4.8 | all-reduce | flops 1280 | bytes 10240 | tf_op jit(solution)/shard_map/psum | solution.py:39
  1096.8 0.7 cholesky.224
  1097.6 0.6 compare_reduce_fusion.1
  1098.3 0.6 fusion.62
  1098.9 0.6 custom-call.28
  1100.1 0.7 cholesky.235
  1100.9 0.6 compare_reduce_fusion
  1101.5 0.6 fusion.63
  1102.2 0.6 custom-call.29
  1103.3 1.5 cholesky.202
  1104.8 0.6 compare_reduce_fusion.3
  1105.5 0.6 fusion.48
  1106.2 1.2 custom-call.26
  1108.0 1.5 cholesky.213
  1109.5 0.6 compare_reduce_fusion.2
  1110.1 0.6 fusion.49
  1110.8 1.2 custom-call.27
  1112.2 6.9 fusion.10
  1119.1 4.2 fusion.8
  1123.3 3.2 copy.97
  1127.7 11.7 cholesky.180
  1139.5 0.6 compare_reduce_fusion.5
  1140.1 0.7 fusion.33
  1140.8 9.8 custom-call.24
  1151.8 11.7 cholesky.191
  1163.5 0.6 compare_reduce_fusion.4
  1164.2 0.7 fusion.34
  1164.9 10.0 custom-call.25
  1175.2 28.3 %reduce-scatter.3.cloned.1.call-done = f32[4,8,2,32,128]{4,3,2,1,0:T(8,128)} async-done(((f32[16,8,2,32,128]{4,3,2,1,0:T(8,128)}), f32[4,8,2,32,128]{4,3,2,1,0:T(8,128)}) %reduce-scatter.3.cloned.1.call-update) | async-done | bytes 1048592 | tf_op jit(solution)/shard_map/reduce_scatter | solution.py:49
  1203.4 6.6 fusion.45
  1210.2 0.7 copy.98
  1210.9 0.6 dynamic-slice_bitcast_fusion.1
  1211.5 50.3 %reduce-scatter.5.cloned.1.call-done = f32[16,4,8,2,128]{4,0,3,2,1:T(8,128)} async-done(((f32[128,4,8,2,128]{4,0,3,2,1:T(8,128)}), f32[16,4,8,2,128]{4,0,3,2,1:T(8,128)}) %reduce-scatter.5.cloned.1.call-update) | async-done | bytes 524304 | tf_op jit(solution)/shard_map/reduce_scatter | solution.py:56
  1261.8 2.1 copy.99
  (67 shorter events, 6.9 us)
Async XLA Ops:
  7.2 786.8 %copy-start = (f32[512,128]{1,0:T(8,128)S(1)}, f32[512,128]{1,0:T(8,128)}, u32[]{:S(2)}) copy-start(f32[512,128]{1,0:T(8,128)} %param.17) | copy-start | bytes 786436
  124.6 190.3 %all-to-all-start = ((f32[8,1,524288]{2,1,0:T(1,128)}), f32[8,1,524288]{2,1,0:T(1,128)}, u32[]{:S(2)}, u32[]{:S(2)}) async-start(f32[8,1,524288]{2,1,0:T(1,128)} %reshape.45), calls=%async_computation | async-start | bytes 33554432 | tf_op jit(solution)/shard_map/all_to_all | solution.py:34
  314.9 549.1 %all-to-all-start.1 = ((f32[4,1,1048576]{2,1,0:T(1,128)}), f32[4,1,1048576]{2,1,0:T(1,128)}, u32[]{:S(2)}, u32[]{:S(2)}) async-start(f32[4,1,1048576]{2,1,0:T(1,128)} %reshape.47), calls=%async_computation.1 | async-start | bytes 33554432 | tf_op jit(solution)/shard_map/all_to_all | solution.py:38
  322.1 471.9 %all-reduce.4.cloned.1.call-start = ((), (), s32[]{:S(2)}) async-start(), calls=%async_computation.6 | async-start | bytes 2621440 | tf_op jit(solution)/shard_map/psum | solution.py:31
  545.5 657.9 %reduce-scatter.3.cloned.1.call-start = ((), (), s32[]{:S(2)}) async-start(), calls=%async_computation.4 | async-start | bytes 5242880 | tf_op jit(solution)/shard_map/reduce_scatter | solution.py:49
  1037.3 59.2 %copy-start.6 = (f32[16,8]{0,1:T(8,128)S(1)}, f32[16,8]{0,1:T(8,128)}, u32[]{:S(2)}) copy-start(f32[16,8]{0,1:T(8,128)} %param.20) | copy-start | bytes 1540
  1037.3 65.7 %copy-start.5 = (f32[32,16]{0,1:T(8,128)S(1)}, f32[32,16]{0,1:T(8,128)}, u32[]{:S(2)}) copy-start(f32[32,16]{0,1:T(8,128)} %param.19) | copy-start | bytes 6148
  1056.9 69.9 %copy-start.1 = (f32[256,256]{1,0:T(8,128)S(1)}, f32[256,256]{1,0:T(8,128)}, u32[]{:S(2)}) copy-start(f32[256,256]{1,0:T(8,128)} %get-tuple-element.35) | copy-start | bytes 786436
  1057.0 69.9 %copy-start.2 = (f32[256,128]{1,0:T(8,128)S(1)}, f32[256,128]{1,0:T(8,128)}, u32[]{:S(2)}) copy-start(f32[256,128]{1,0:T(8,128)} %param.18) | copy-start | bytes 393220
  1103.0 107.1 %copy-start.4 = (f32[8,16]{1,0:T(8,128)}, f32[8,16]{1,0:T(8,128)S(1)}, u32[]{:S(2)}) copy-start(f32[8,16]{1,0:T(8,128)S(1)} %fusion.64) | copy-start | bytes 1540
  1112.2 97.9 %copy-start.3 = (f32[16,32]{1,0:T(8,128)}, f32[16,32]{1,0:T(8,128)S(1)}, u32[]{:S(2)}) copy-start(f32[16,32]{1,0:T(8,128)S(1)} %fusion.51) | copy-start | bytes 6148
  1126.5 135.2 %reduce-scatter.5.cloned.1.call-start = ((), (), s32[]{:S(2)}) async-start(), calls=%async_computation.5 | async-start | bytes 4718592 | tf_op jit(solution)/shard_map/reduce_scatter | solution.py:56
Sparse Core Ops, SparseCore 0:
  545.6 248.3 all-reduce.3
  1126.7 76.7 reduce-scatter.2
  1210.2 51.5 reduce-scatter.4
where the time goes:
time: 1280 us; the launch traced here: 1270 us
  local copies, waits for them, and re-layouts  408 us (32%)
  waiting for transfers between devices  400 us (31%)
  other arithmetic  210 us (16%)
  matrix products  185 us (14%)
  blocking collectives  39.5 us (3%)
  between operations  14.6 us (1%)
  starting transfers between devices  13.3 us (1%)
    unnamed x21, local copies, waits for them, and re-layouts  312 us
    psum x1, waiting for transfers between devices, shards(): gram_in, gram_y = lax.psum((gram_in_part, gram_y_part), ('fsdp', 'mode'))  197 us
    all_to_all x1, waiting for transfers between devices, shards(): lax.all_to_all(gradient, 'fsdp', split_axis=4, concat_axis=3, tiled=True)  124 us
    another operation x24, other arithmetic, sweeps(): lower_factor = jnp.linalg.cholesky(inner)  56.9 us
    all_to_all x1, other arithmetic, shards(): lax.all_to_all(gradient, 'mode', split_axis=4, concat_axis=0, tiled=True)  54.5 us
    dot_general x1, matrix products, shards(): jnp.einsum('xycoi,xzcoi->yz', gradient, gradient, precision=precise)  51.9 us
    all_to_all x1, other arithmetic, shards(): lax.all_to_all(gradient, 'fsdp', split_axis=4, concat_axis=3, tiled=True)  50.6 us
    reduce_scatter x1, waiting for transfers between devices, shards(): lax.psum_scatter(jnp.einsum('pqcoa,ob->bpqca', partial_core, columns, pre...  50.3 us
  transfers between devices with their start and end apart: 5, of which 4 were waited for; matrix products, arithmetic and copies ran while one was open for 36% of the time, Pallas kernels for 0%

commit v1 on v0

--- a/solution.py
+++ b/solution.py
@@ -31,7 +31,10 @@
     gram_in, gram_y = lax.psum((gram_in_part, gram_y_part), ("fsdp", "mode"))
     full_in = sweeps(gram_in, start_in)
     factor_y = sweeps(gram_y, start_y)
-    by_out = lax.all_to_all(gradient, "fsdp", split_axis=4, concat_axis=3, tiled=True)
+    by_out = jnp.concatenate(
+        lax.all_to_all(jnp.stack(jnp.split(gradient, lax.axis_size("fsdp"), axis=4)), "fsdp", 0, 0),
+        axis=3,
+    )
     gram_out = lax.psum(
         jnp.einsum("xycoi,xycpi->op", by_out, by_out, precision=precise), ("fsdp", "mode")
     )

time: 1280 us -> 1220 us (0.953)
  local copies, waits for them, and re-layouts: 408 us -> 345 us
    psum x1, waiting for transfers between devices: 197 us -> 249 us  [shards(): gram_in, gram_y = lax.psum((gram_in_part, gram_y_part), ('fsdp', 'mode'))]
    all_to_all x1, waiting for transfers between devices: 124 us -> 74 us  [shards(): lax.all_to_all(jnp.stack(jnp.split(gradient, lax.axis_size('fsdp'), axis=...]
    all_to_all x2 -> x1, local copies, waits for them, and re-layouts: 49 us -> 0.51 us  [shards(): lax.all_to_all(jnp.stack(jnp.split(gradient, lax.axis_size('fsdp'), axis=...]
    unnamed x21 -> x30, local copies, waits for them, and re-layouts: 312 us -> 270 us
    reshape x0 -> x1, local copies, waits for them, and re-layouts: none -> 23.5 us  [shards(): jnp.concatenate(lax.all_to_all(jnp.stack(jnp.split(gradient, lax.axis_siz...]
  transfers between devices with their start and end apart: 5 -> 5, of which waited for: 4 -> 4; matrix products, arithmetic and copies ran while one was open for 36% -> 37% of each run, Pallas kernels for 0% -> 0%
where the time goes in v1:
time: 1220 us; the launch traced here: 1210 us
  waiting for transfers between devices  402 us (33%)
  local copies, waits for them, and re-layouts  345 us (28%)
  other arithmetic  210 us (17%)
  matrix products  183 us (15%)
  blocking collectives  39.5 us (3%)
  between operations  14.6 us (1%)
  starting transfers between devices  13.7 us (1%)
    unnamed x30, local copies, waits for them, and re-layouts  270 us
    psum x1, waiting for transfers between devices, shards(): gram_in, gram_y = lax.psum((gram_in_part, gram_y_part), ('fsdp', 'mode'))  249 us
    all_to_all x1, waiting for transfers between devices, shards(): lax.all_to_all(jnp.stack(jnp.split(gradient, lax.axis_size('fsdp'), axis=...  74 us
    another operation x24, other arithmetic, sweeps(): lower_factor = jnp.linalg.cholesky(inner)  56.9 us
    all_to_all x1, other arithmetic, shards(): lax.all_to_all(gradient, 'mode', split_axis=4, concat_axis=0, tiled=True)  54.5 us
    dot_general x1, matrix products, shards(): jnp.einsum('xycoi,xzcoi->yz', gradient, gradient, precision=precise)  52.1 us
    reduce_scatter x1, waiting for transfers between devices, shards(): lax.psum_scatter(jnp.einsum('pqcoa,ob->bpqca', partial_core, columns, pre...  50.3 us
    all_to_all x1, other arithmetic, shards(): lax.all_to_all(jnp.stack(jnp.split(gradient, lax.axis_size('fsdp'), axis=...  50.2 us
  transfers between devices with their start and end apart: 5, of which 4 were waited for; matrix products, arithmetic and copies ran while one was open for 37% of the time, Pallas kernels for 0%

profile of v1, /device:TPU:0, one launch (start us, length us, event | category | flops | bytes accessed | tf_op | source)
XLA Modules:
  0.0 1207.6 jit_solution(16921655623508789209)
XLA Ops:
  7.2 5.3 bitcast_dynamic-update-slice_fusion.7
  12.5 6.1 bitcast_dynamic-update-slice_fusion.6
  18.6 2.6 bitcast_dynamic-update-slice_fusion.5
  21.2 3.1 bitcast_dynamic-update-slice_fusion.4
  24.3 2.5 bitcast_dynamic-update-slice_fusion.3
  26.8 3.1 bitcast_dynamic-update-slice_fusion.2
  29.9 2.6 bitcast_dynamic-update-slice_fusion.1
  32.5 3.1 bitcast_dynamic-update-slice_fusion
  35.6 25.5 %reshape.53 = f32[8,1,524288]{2,1,0:T(1,128)} reshape(f32[8,8,16,2,32,64]{5,4,3,2,1,0:T(8,128)} %bitcast_dynamic-update-slice_fusion) | data formatting | bytes 33554432
  61.1 5.9 all-to-all-start
  67.0 50.4 %copy.82 = f32[8,16,2,32,512]{3,1,2,0,4:T(8,128)} copy(f32[8,16,2,32,512]{4,3,2,1,0:T(8,128)} %param.16) | data formatting | bytes 33554432 | tf_op args[0]
  117.4 60.2 %reshape.55 = f32[4,1,1048576]{2,1,0:T(1,128)} reshape(f32[512,8,2,16,32]{4,3,2,1,0:T(8,128)} %bitcast.169) | data formatting | bytes 33554432
  177.6 74.0 %all-to-all-done = f32[8,1,524288]{2,1,0:T(1,128)} async-done(((f32[8,1,524288]{2,1,0:T(1,128)}), f32[8,1,524288]{2,1,0:T(1,128)}, u32[]{:S(2)}, u32[]{:S(2)}) %all-to-all-start) | async-done | bytes 16777248 | tf_op jit(solution)/shard_map/all_to_all | solution.py:35
  251.6 7.0 all-to-all-start.1
  259.1 31.6 %fusion.15 = f32[512,512]{1,0:T(8,128)} fusion(f32[8,16,2,32,512]{4,3,2,1,0:T(8,128)} %param.16), kind=kOutput, calls=%fused_computation.22 | convolution fusion | flops 25769803776 | bytes 17825792 | tf_op jit(solution)/shard_map/xycoi,xycoj->ij/dot_general | solution.py:30
  291.2 50.2 %reduce.12 = f32[8,524288]{1,0:T(8,128)} reduce(f32[8,1,524288]{2,1,0:T(1,128)} %all-to-all-done, f32[]{:T(128)} %broadcast.120), dimensions={1}, to_apply=%all_to_all.16.reduce_sub_computation | reduce | bytes 33554436 | tf_op jit(solution)/shard_map/all_to_all | solution.py:35
  341.4 30.2 %reshape.54 = f32[8,8,16,2,32,64]{5,4,3,2,1,0:T(8,128)} reshape(f32[8,524288]{1,0:T(8,128)} %reduce.12) | data formatting | bytes 33554432
  371.6 23.5 %copy.77 = f32[8,16,2,8,32,64]{5,4,3,2,1,0:T(8,128)} copy(f32[8,16,2,8,32,64]{5,4,2,1,0,3:T(8,128)} %bitcast.206) | data formatting | bytes 33554432 | tf_op jit(solution)/shard_map/reshape | solution.py:34
  395.1 34.2 %fusion.18 = f32[256,256]{1,0:T(8,128)} fusion(f32[8,16,2,256,64]{4,3,2,1,0:T(8,128)} %bitcast.205), kind=kOutput, calls=%fused_computation.23 | convolution fusion | flops 12884901888 | bytes 17039360 | tf_op jit(solution)/shard_map/xycoi,xycpi->op/dot_general | solution.py:39
  429.5 52.1 %fusion.24 = f32[16,16]{1,0:T(8,128)S(1)} fusion(f32[8,16,2,32,512]{4,3,2,1,0:T(8,128)} %param.16), kind=kOutput, calls=%fused_computation.25 | convolution fusion | flops 805306368 | bytes 16778240 | tf_op jit(solution)/shard_map/xycoi,xzcoi->yz/dot_general | solution.py:29
  481.6 249.2 %all-reduce.4.cloned.1.call-done = (f32[512,512]{1,0:T(8,128)}, f32[256,256]{1,0:T(8,128)}) async-done(((f32[512,512]{1,0:T(8,128)}, f32[256,256]{1,0:T(8,128)}), (f32[512,512]{1,0:T(8,128)}, f32[256,256]{1,0:T(8,128)})) %all-reduce.4.cloned.1.call-update) | async-done | bytes 1310736 | tf_op jit(solution)/shard_map/psum | solution.py:31
  730.7 2.2 fusion.82
  733.6 11.7 cholesky.158
  745.4 0.6 compare_reduce_fusion.7
  746.0 0.7 fusion.36
  746.7 9.8 custom-call.22
  756.9 2.2 fusion.84
  759.9 11.9 cholesky.169
  772.5 0.7 fusion.37
  773.1 9.8 custom-call.23
  783.4 17.3 %convolution_bitcast_fusion = f32[8,16,2,32,128]{4,3,2,1,0:T(8,128)} fusion(f32[8,16,2,32,512]{4,3,2,1,0:T(8,128)} %param.16, f32[128,512]{1,0:T(8,128)S(1)} %fusion.28), kind=kOutput, calls=%fused_computation.18 | convolution fusion | flops 6442450944 | bytes 21233664 | tf_op jit(solution)/shard_map/xycoi,ia->xycoa/dot_general | solution.py:47
  800.7 54.5 %reduce.13 = f32[4,1048576]{1,0:T(4,128)} reduce(f32[4,1,1048576]{2,1,0:T(1,128)} %all-to-all-done.1, f32[]{:T(128)} %broadcast.120), dimensions={1}, to_apply=%all_to_all.17.reduce_sub_computation | reduce | bytes 33554436 | tf_op jit(solution)/shard_map/all_to_all | solution.py:41
  855.2 76.0 %reshape.56 = f32[512,8,2,16,32]{4,3,2,1,0:T(8,128)} reshape(f32[4,1048576]{1,0:T(4,128)} %reduce.13) | data formatting | bytes 33554432
  931.2 42.8 %copy.83 = f32[8,16,2,32,4,128]{5,0,4,1,3,2:T(8,128)} copy(f32[8,16,2,32,4,128]{3,1,2,0,5,4:T(8,128)} %bitcast.32) | data formatting | bytes 33554432 | tf_op jit(solution)/shard_map/all_to_all | solution.py:41
  974.0 19.6 %fusion.21 = f32[32,32]{1,0:T(8,128)S(1)} fusion(f32[8,16,2,32,4,128]{5,0,4,1,3,2:T(8,128)} %copy.83), kind=kOutput, calls=%fused_computation.24 | convolution fusion | flops 1610612736 | bytes 16781312 | tf_op jit(solution)/shard_map/xycoi,zycoi->xz/dot_general | solution.py:43
  993.7 39.5 %all-reduce = (f32[32,32]{1,0:T(8,128)S(1)}, f32[16,16]{1,0:T(8,128)S(1)}) all-reduce(f32[32,32]{1,0:T(8,128)S(1)} %fusion.21, f32[16,16]{1,0:T(8,128)S(1)} %fusion.24), channel_id=1, replica_groups=mesh['fsdp'=8,'mode'=4] {'fsdp','mode'}, use_global_device_ids=true, to_apply=%region_4.8 | all-reduce | flops 1280 | bytes 10240 | tf_op jit(solution)/shard_map/psum | solution.py:42
  1033.5 0.7 cholesky.224
  1034.3 0.6 compare_reduce_fusion.1
  1034.9 0.6 fusion.67
  1036.8 0.7 cholesky.235
  1037.5 0.6 compare_reduce_fusion
  1038.2 0.6 fusion.68
  1040.0 1.5 cholesky.202
  1041.5 0.6 compare_reduce_fusion.3
  1042.2 0.6 fusion.53
  1042.8 1.2 custom-call.26
  1044.7 1.5 cholesky.213
  1046.2 0.6 compare_reduce_fusion.2
  1046.8 0.6 fusion.54
  1047.5 1.2 custom-call.27
  1048.9 6.9 fusion.12
  1055.8 4.2 fusion.10
  1060.0 3.2 copy.95
  1064.4 11.7 cholesky.180
  1076.8 0.7 fusion.38
  1077.5 9.8 custom-call.24
  1088.5 11.7 cholesky.191
  1100.9 0.7 fusion.39
  1101.5 10.0 custom-call.25
  1111.9 28.3 %reduce-scatter.3.cloned.1.call-done = f32[4,8,2,32,128]{4,3,2,1,0:T(8,128)} async-done(((f32[16,8,2,32,128]{4,3,2,1,0:T(8,128)}), f32[4,8,2,32,128]{4,3,2,1,0:T(8,128)}) %reduce-scatter.3.cloned.1.call-update) | async-done | bytes 1048592 | tf_op jit(solution)/shard_map/reduce_scatter | solution.py:52
  1140.1 6.6 fusion.50
  1146.9 0.7 copy.96
  1148.2 50.3 %reduce-scatter.5.cloned.1.call-done = f32[16,4,8,2,128]{4,0,3,2,1:T(8,128)} async-done(((f32[128,4,8,2,128]{4,0,3,2,1:T(8,128)}), f32[16,4,8,2,128]{4,0,3,2,1:T(8,128)}) %reduce-scatter.5.cloned.1.call-update) | async-done | bytes 524304 | tf_op jit(solution)/shard_map/reduce_scatter | solution.py:59
  1198.5 2.1 copy.97
  (77 shorter events, 12.3 us)
Async XLA Ops:
  7.2 723.6 %copy-start = (f32[512,128]{1,0:T(8,128)S(1)}, f32[512,128]{1,0:T(8,128)}, u32[]{:S(2)}) copy-start(f32[512,128]{1,0:T(8,128)} %param.17) | copy-start | bytes 786436
  7.2 11.4 copy-start.1
  61.1 190.5 %all-to-all-start = ((f32[8,1,524288]{2,1,0:T(1,128)}), f32[8,1,524288]{2,1,0:T(1,128)}, u32[]{:S(2)}, u32[]{:S(2)}) async-start(f32[8,1,524288]{2,1,0:T(1,128)} %reshape.53), calls=%async_computation | async-start | bytes 33554432 | tf_op jit(solution)/shard_map/all_to_all | solution.py:35
  251.6 549.1 %all-to-all-start.1 = ((f32[4,1,1048576]{2,1,0:T(1,128)}), f32[4,1,1048576]{2,1,0:T(1,128)}, u32[]{:S(2)}, u32[]{:S(2)}) async-start(f32[4,1,1048576]{2,1,0:T(1,128)} %reshape.55), calls=%async_computation.1 | async-start | bytes 33554432 | tf_op jit(solution)/shard_map/all_to_all | solution.py:41
  258.6 472.1 %all-reduce.4.cloned.1.call-start = ((), (), s32[]{:S(2)}) async-start(), calls=%async_computation.6 | async-start | bytes 2621440 | tf_op jit(solution)/shard_map/psum | solution.py:31
  429.4 710.7 %reduce-scatter.3.cloned.1.call-start = ((), (), s32[]{:S(2)}) async-start(), calls=%async_computation.4 | async-start | bytes 5242880 | tf_op jit(solution)/shard_map/reduce_scatter | solution.py:52
  974.0 59.2 %copy-start.7 = (f32[16,8]{0,1:T(8,128)S(1)}, f32[16,8]{0,1:T(8,128)}, u32[]{:S(2)}) copy-start(f32[16,8]{0,1:T(8,128)} %param.20) | copy-start | bytes 1540
  974.0 65.7 %copy-start.6 = (f32[32,16]{0,1:T(8,128)S(1)}, f32[32,16]{0,1:T(8,128)}, u32[]{:S(2)}) copy-start(f32[32,16]{0,1:T(8,128)} %param.19) | copy-start | bytes 6148
  993.7 69.9 %copy-start.2 = (f32[256,256]{1,0:T(8,128)S(1)}, f32[256,256]{1,0:T(8,128)}, u32[]{:S(2)}) copy-start(f32[256,256]{1,0:T(8,128)} %get-tuple-element.35) | copy-start | bytes 786436
  993.7 69.9 %copy-start.3 = (f32[256,128]{1,0:T(8,128)S(1)}, f32[256,128]{1,0:T(8,128)}, u32[]{:S(2)}) copy-start(f32[256,128]{1,0:T(8,128)} %param.18) | copy-start | bytes 393220
  1039.7 107.1 %copy-start.5 = (f32[8,16]{1,0:T(8,128)}, f32[8,16]{1,0:T(8,128)S(1)}, u32[]{:S(2)}) copy-start(f32[8,16]{1,0:T(8,128)S(1)} %fusion.69) | copy-start | bytes 1540
  1048.9 97.9 %copy-start.4 = (f32[16,32]{1,0:T(8,128)}, f32[16,32]{1,0:T(8,128)S(1)}, u32[]{:S(2)}) copy-start(f32[16,32]{1,0:T(8,128)S(1)} %fusion.56) | copy-start | bytes 6148
  1063.2 135.3 %reduce-scatter.5.cloned.1.call-start = ((), (), s32[]{:S(2)}) async-start(), calls=%async_computation.5 | async-start | bytes 4718592 | tf_op jit(solution)/shard_map/reduce_scatter | solution.py:59
Sparse Core Ops, SparseCore 0:
  429.5 301.1 all-reduce.3
  1063.4 76.7 reduce-scatter.2
  1146.9 51.5 reduce-scatter.4
